TPU v7x, 128 devices: a whole 4x4x4 slice. The times are simulated.
128 devices in a mesh: store: 16 (over x, y), ctx: 8 (over z, core).
Axes of the slice: x: 4, y: 4, z: 4, core: 2. Of those that a mesh axis runs over, the one named last changes fastest.
Arguments:
- tokens: bfloat16 [2048, 8192], P('store'), may hold values from -6 to 6
- joined_weight: bfloat16 [8192, 8, 1280], P(None, 'ctx'), may hold values from -0.0625 to 0.0625
- down_weight: bfloat16 [128, 8192, 64], P('store', 'ctx'), may hold values from -0.0625 to 0.0625
- up_weight: bfloat16 [128, 64, 8, 1280], P('store', None, 'ctx'), may hold values from -0.75 to 0.75
- adapter_per_request: int32 [2048], replicated, may hold values from 0 to 127, as said below
- adapter_store_slot: int32 [128], replicated, may hold values from 0 to 127, as said below
- prefix_block_list: int32 [2048, 8], P('store'), may hold values from 0 to 255, as said below
- prefix_length: int32 [2048], P('store'), may hold values from 1 to 128, as said below
- key_value_pool: bfloat16 [4096, 8, 256], P(('store', 'ctx')), may hold values from -400 to 400
Outputs:
- attn: bfloat16 [2048, 8, 1024], P('store', 'ctx')
Inputs may be any that keep to these rules, and one draw needn't show every extreme that they name: `adapter_store_slot`: A permutation; slot s belongs to owner s // 8, which holds slots in store order. `adapter_per_request`: among the 128 requests of one store shard, at most 16 use adapters of one owner; on every shard one owner, the same for all shards, receives exactly 16. `prefix_block_list`: the 8 blocks of a request are distinct and lie in its store shard's range of 16 blocks, rows i * 128 to (i+1) * 128 - 1 using blocks i * 16 to (i+1) * 16 - 1. `prefix_length`: every store shard has a request of length 128.
All inputs are finite; a program needn't handle non-finite values.
Results may differ from a plain program's by a relative error of at most 0.02.
The roundings to bfloat16 on the way count: a program that leaves them out, or rounds other values in their place, can miss the bound.
Values may be sent and summed in bfloat16 or wider, within the bound.
No kernel may reach another device: no remote copies, remote signals or barrier semaphores. Data moves between devices by JAX's collectives and lax.ppermute only.
A program may use at most 128 MiB of HBM per device.

v0:
```python
import jax
import jax.numpy as jnp
from jax import lax
from jax.sharding import PartitionSpec as P

QUERY_PER_KEY = 8
HEAD_SIZE = 128
CAP = 16
BLK = 16
ROPE_THETA = 500000.0
ADAPTER_SCALE = 2.0


def rotary_apply(vec, token_position):
    half = vec.shape[-1] // 2
    freq = jnp.power(ROPE_THETA, -(jnp.arange(half, dtype=jnp.float32) * 2.0 / vec.shape[-1]))
    angle = token_position[..., None] * freq
    cosine = jnp.cos(angle)
    sine = jnp.sin(angle)
    initial_part = vec[..., :half]
    second = vec[..., half:]
    return jnp.concatenate(
        [initial_part * cosine - second * sine, initial_part * sine + second * cosine], axis=-1
    )


def prefix_mask(local_ids, lens, group_blocks, blk):
    listed = local_ids.shape[1]
    equal = local_ids[:, :, None] == jnp.arange(group_blocks, dtype=jnp.int32)[None, None, :]
    start = jnp.sum(
        jnp.where(equal, (jnp.arange(listed, dtype=jnp.int32) * blk)[None, :, None], 0), axis=1
    )
    present = jnp.any(equal, axis=1)
    offset = jnp.arange(blk, dtype=jnp.int32)
    live = present[:, :, None] & (start[:, :, None] + offset[None, None, :] < lens[:, None, None])
    return live.reshape(local_ids.shape[0], group_blocks * blk)


def attend(query_rows, key_new, value_new, keys, value_rows, live):
    scale = 1.0 / HEAD_SIZE**0.5
    pool_scores = (
        jnp.einsum("rhgd,thd->rhgt", query_rows, keys, preferred_element_type=jnp.float32) * scale
    )
    own = (
        jnp.einsum("rhgd,rhd->rhg", query_rows, key_new, preferred_element_type=jnp.float32) * scale
    )
    mask = live[:, None, None, :]
    pool_scores = jnp.where(mask, pool_scores, -jnp.inf)
    top = jnp.maximum(jnp.max(pool_scores, axis=-1), own)
    prob = jnp.where(mask, jnp.exp(pool_scores - top[..., None]), 0.0)
    prob_own = jnp.exp(own - top)
    total = jnp.sum(prob, axis=-1) + prob_own
    prob_low = prob.astype(jnp.bfloat16)
    own_low = prob_own.astype(jnp.bfloat16)
    mixed = jnp.einsum("rhgt,thd->rhgd", prob_low, value_rows, preferred_element_type=jnp.float32)
    mixed = (
        mixed
        + own_low.astype(jnp.float32)[..., None] * value_new.astype(jnp.float32)[:, :, None, :]
    )
    mixed = mixed / total[..., None]
    return mixed.astype(jnp.bfloat16).reshape(query_rows.shape[0], query_rows.shape[1], -1)


def routing(adapter_per_request, adapter_store_slot, shards, request_shard, shard_adapters):
    adapters = adapter_store_slot.shape[0]
    match = adapter_per_request[:, None] == jnp.arange(adapters, dtype=jnp.int32)[None, :]
    store_slot = jnp.sum(jnp.where(match, adapter_store_slot[None, :], 0), axis=1).reshape(
        shards, request_shard
    )
    owner = store_slot // shard_adapters
    owner_hot = (owner[:, :, None] == jnp.arange(shards, dtype=jnp.int32)[None, None, :]).astype(
        jnp.int32
    )
    counted = jnp.cumsum(owner_hot, axis=1) - 1
    rank = jnp.sum(owner_hot * counted, axis=2)
    return (store_slot, owner, rank)


def body(
    tokens,
    joined_weight,
    down_weight,
    up_weight,
    adapter_per_request,
    adapter_store_slot,
    prefix_block_list,
    prefix_length,
    key_value_pool,
):
    n_store = lax.axis_size("store")
    n_ctx = lax.axis_size("ctx")
    shard = lax.axis_index("store")
    member = lax.axis_index("ctx")
    request_shard = tokens.shape[0]
    d_model = tokens.shape[1]
    shard_adapters = down_weight.shape[0]
    width_slice = down_weight.shape[1]
    head_slice = joined_weight.shape[1]
    column_list = joined_weight.shape[2]
    whole_group = lax.all_gather(key_value_pool, "ctx", axis=0, tiled=True)
    group = lax.dynamic_slice_in_dim(whole_group, member * head_slice, head_slice, 1)
    store_slot, owner, rank = routing(
        adapter_per_request, adapter_store_slot, n_store, request_shard, shard_adapters
    )
    owner_mine = lax.dynamic_index_in_dim(owner, shard, 0, keepdims=False)
    rank_mine = lax.dynamic_index_in_dim(rank, shard, 0, keepdims=False)
    dest = owner_mine * CAP + rank_mine
    x_local = lax.dynamic_slice_in_dim(tokens, member * width_slice, width_slice, 1)
    outgoing = jnp.zeros((n_store * CAP, width_slice), jnp.bfloat16).at[dest].set(x_local)
    received_parts = lax.all_to_all(
        outgoing.reshape(n_store, CAP, width_slice),
        "store",
        split_axis=0,
        concat_axis=0,
        tiled=True,
    )
    local_slot = store_slot % shard_adapters
    selected = (owner == shard)[:, :, None] & (
        rank[:, :, None] == jnp.arange(CAP, dtype=jnp.int32)[None, None, :]
    )
    adapter_hot = selected[:, :, :, None] & (
        local_slot[:, :, None, None]
        == jnp.arange(shard_adapters, dtype=jnp.int32)[None, None, None, :]
    )
    adapter_hot = jnp.any(adapter_hot, axis=1)
    value_partial = jnp.einsum(
        "hbm,gmq->hbgq", received_parts, down_weight, preferred_element_type=jnp.float32
    )
    shrunk_part = jnp.sum(jnp.where(adapter_hot[..., None], value_partial, 0.0), axis=2)
    shrunk = lax.psum(shrunk_part, "ctx").astype(jnp.bfloat16)
    spread_rows = jnp.where(
        adapter_hot[..., None], shrunk[:, :, None, :], jnp.zeros((), jnp.bfloat16)
    )
    adapter_update = jnp.einsum(
        "oxbl,blpj->oxpj", spread_rows, up_weight, preferred_element_type=jnp.float32
    ).astype(jnp.bfloat16)
    returned = lax.all_to_all(adapter_update, "store", split_axis=0, concat_axis=0, tiled=True)
    update_mine = returned.reshape(n_store * CAP, head_slice, column_list)[dest]
    plain_projection = jnp.dot(
        tokens,
        joined_weight.reshape(d_model, head_slice * column_list),
        preferred_element_type=jnp.float32,
    )
    joined_projection = plain_projection.reshape(
        request_shard, head_slice, column_list
    ) + ADAPTER_SCALE * update_mine.astype(jnp.float32)
    token_position = prefix_length.astype(jnp.float32)
    query_rows = rotary_apply(
        joined_projection[:, :, : QUERY_PER_KEY * HEAD_SIZE].reshape(
            request_shard, head_slice, QUERY_PER_KEY, HEAD_SIZE
        ),
        token_position[:, None, None],
    ).astype(jnp.bfloat16)
    key_new = rotary_apply(
        joined_projection[:, :, QUERY_PER_KEY * HEAD_SIZE : (QUERY_PER_KEY + 1) * HEAD_SIZE],
        token_position[:, None],
    ).astype(jnp.bfloat16)
    value_new = joined_projection[:, :, (QUERY_PER_KEY + 1) * HEAD_SIZE :].astype(jnp.bfloat16)
    group_blocks = key_value_pool.shape[0] * n_ctx // BLK
    live = prefix_mask(prefix_block_list - shard * group_blocks, prefix_length, group_blocks, BLK)
    return attend(
        query_rows, key_new, value_new, group[:, :, :HEAD_SIZE], group[:, :, HEAD_SIZE:], live
    )


def solution(mesh):
    in_specs = (
        P("store", None),
        P(None, "ctx", None),
        P("store", "ctx", None),
        P("store", None, "ctx", None),
        P(),
        P(),
        P("store", None),
        P("store"),
        P(("store", "ctx"), None, None),
    )
    out_specs = P("store", "ctx", None)
    return jax.shard_map(body, mesh=mesh, in_specs=in_specs, out_specs=out_specs, check_vma=False)
```

profile of v0, /device:TPU:0, one launch (start us, length us, event | category | flops | bytes accessed | tf_op | source)
XLA Modules:
  0.0 103.6 jit_solution(7977212411898777867)
XLA Ops:
  6.5 1.7 %copy.72 = bf16[32,8,256]{2,0,1:T(8,128)(2,1)} copy(bf16[32,8,256]{2,1,0:T(8,128)(2,1)} %param.17) | data formatting | bytes 262144 | tf_op args[8]
  8.3 1.3 %select_reduce_fusion.1 = s32[2048]{0:T(1024)S(1)} fusion(s32[128]{0:T(128)} %param.14, s32[2048]{0:T(1024)} %param.13), kind=kLoop, calls=%fused_computation.25 | loop fusion | flops 784384 | bytes 16896 | tf_op jit(solution)/shard_map/reduce_sum | solution.py:67
  9.8 2.8 %select_reduce_fusion = s32[16,128]{0,1:T(8,128)S(1)} fusion(s32[16,128]{0,1:T(8,128)S(1)} %copy.73), kind=kOutput, calls=%fused_computation.21 | output fusion | flops 4356096 | bytes 16384 | tf_op jit(solution)/shard_map/jit(cumsum)/reduce_window_sum | solution.py:74
  12.7 2.0 %scatter_custom_fusion = bf16[256,1024]{1,0:T(8,128)(2,1)} fusion(s32[128]{0:T(128)S(1)} %fusion.66, bf16[128,8192]{1,0:T(8,128)(2,1)S(1)} %copy-done, s32[]{:T(128)} %constant.35.clone.1, s32[]{:T(128)S(6)} %select_n.75, bf16[]{:T(256)} %constant.73.clone.1), kind=kCustom, calls=%fused_computation.46 | custom fusion | bytes 786442 | tf_op jit(solution)/shard_map/scatter | solution.py:109
  14.6 7.1 %all-to-all-start = ((bf16[16,16,1024]{2,1,0:T(8,128)(2,1)}), bf16[16,16,1024]{2,1,0:T(8,128)(2,1)S(1)}, u32[]{:S(2)}, u32[]{:S(2)}) async-start(bf16[16,16,1024]{2,1,0:T(8,128)(2,1)} %bitcast.10), calls=%async_computation | async-start | bytes 1048576 | tf_op jit(solution)/shard_map/all_to_all | solution.py:110
  21.9 4.4 %and_reduce_fusion = pred[16,16,8]{2,1,0:T(8,128)(4,1)S(1)} fusion(pred[16,128,8]{1,2,0:T(8,128)(4,1)S(1)} %iota_compare_fusion.4, pred[16,128,16]{1,2,0:T(8,128)(4,1)S(1)} %fusion.41), kind=kLoop, calls=%fused_computation.27 | loop fusion | flops 522240 | bytes 51200 | tf_op jit(solution)/shard_map/reduce_or | solution.py:125
  26.5 6.8 %all-to-all-done = bf16[16,16,1024]{2,1,0:T(8,128)(2,1)S(1)} async-done(((bf16[16,16,1024]{2,1,0:T(8,128)(2,1)}), bf16[16,16,1024]{2,1,0:T(8,128)(2,1)S(1)}, u32[]{:S(2)}, u32[]{:S(2)}) %all-to-all-start) | async-done | bytes 524320 | tf_op jit(solution)/shard_map/all_to_all | solution.py:110
  33.3 2.0 %fusion.12 = f32[16,16,64]{2,1,0:T(8,128)S(1)} fusion(bf16[8,1024,64]{1,2,0:T(8,128)(2,1)} %param.11, bf16[16,16,1024]{2,1,0:T(8,128)(2,1)S(1)} %all-to-all-done, pred[16,16,8]{1,2,0:T(8,128)(4,1)S(1)} %copy.75), kind=kOutput, calls=%fused_computation.13 | convolution fusion | flops 268681216 | bytes 1640448 | tf_op jit(solution)/shard_map/hbm,gmq->hbgq/dot_general | solution.py:126
  35.3 26.7 %psum.7 = bf16[16,16,64]{2,1,0:T(8,128)(2,1)S(1)} all-reduce(f32[16,16,64]{2,1,0:T(8,128)S(1)} %fusion.12), channel_id=1, replica_groups=mesh['store'=16,'ctx'=8] {'ctx'}, use_global_device_ids=true, to_apply=%region_8.9 | all-reduce | flops 16384 | bytes 98304 | tf_op jit(solution)/shard_map/psum | solution.py:130
  62.0 3.0 %fusion.6 = bf16[16,16,1,1280]{3,1,2,0:T(8,128)(2,1)} fusion(bf16[8,64,1,1280]{3,1,2,0:T(8,128)(2,1)} %param.12, pred[16,16,8]{1,2,0:T(8,128)(4,1)S(1)} %copy.75, bf16[16,16,64]{2,1,0:T(8,128)(2,1)S(1)} %psum.7), kind=kOutput, calls=%fused_computation.7 | convolution fusion | flops 336003072 | bytes 2000896 | tf_op jit(solution)/shard_map/oxbl,blpj->oxpj/dot_general | solution.py:134
  65.0 3.8 %all-to-all-start.1 = ((bf16[16,16,1,1280]{3,1,2,0:T(8,128)(2,1)}), bf16[16,16,1,1280]{3,1,2,0:T(8,128)(2,1)S(1)}, u32[]{:S(2)}, u32[]{:S(2)}) async-start(bf16[16,16,1,1280]{3,1,2,0:T(8,128)(2,1)} %fusion.6), calls=%async_computation.1 | async-start | bytes 1310720 | tf_op jit(solution)/shard_map/all_to_all | solution.py:137
  69.1 0.3 multiply_cosine_fusion.1
  69.4 10.1 %all-to-all-done.1 = bf16[16,16,1,1280]{3,1,2,0:T(8,128)(2,1)S(1)} async-done(((bf16[16,16,1,1280]{3,1,2,0:T(8,128)(2,1)}), bf16[16,16,1,1280]{3,1,2,0:T(8,128)(2,1)S(1)}, u32[]{:S(2)}, u32[]{:S(2)}) %all-to-all-start.1) | async-done | bytes 655392 | tf_op jit(solution)/shard_map/all_to_all | solution.py:137
  79.5 1.6 %gather_fusion = bf16[128,1280]{1,0:T(8,128)(2,1)} fusion(bf16[256,1280]{1,0:T(8,128)(2,1)S(1)} %bitcast.144, s32[1024]{0:T(1024)S(1)} %pad_clamp_fusion), kind=kCustom, calls=%fused_computation | custom fusion | bytes 655872 | tf_op jit(solution)/shard_map/gather | solution.py:138
  81.2 9.9 %fusion.7 = f32[128,1,1280]{2,0,1:T(8,128)S(1)} fusion(bf16[128,8192]{1,0:T(8,128)(2,1)S(1)} %copy-done, bf16[8192,1,1280]{2,0,1:T(8,128)(2,1)} %param.10, bf16[128,1280]{1,0:T(8,128)(2,1)} %gather_fusion), kind=kOutput, calls=%fused_computation.8 | convolution fusion | flops 2684846080 | bytes 24051712 | tf_op jit(solution)/shard_map/dot_general | solution.py:139
  91.2 0.7 copy.82
  91.9 0.3 fusion.56
  92.3 0.2 fusion.69
  92.5 0.2 fusion.31
  92.9 0.3 fusion.38
  93.3 1.2 %fusion.70 = (f32[128,8]{0,1:T(8,128)S(1)}, f32[128,1,8,256]{0,3,2,1:T(8,128)S(1)}) fusion(bf16[128,8,128]{2,0,1:T(8,128)(2,1)S(1)} %pad_maximum_fusion, bf16[256,8,256]{2,0,1:T(8,128)(2,1)} %all-gather.2.cloned.1.call-done, s32[]{:T(128)S(6)} %select_n.68, pred[128,256]{0,1:T(8,128)(4,1)S(1)} %fusion.42), kind=kOutput, calls=%fused_computation.112 | convolution fusion | flops 67894272 | bytes 1413124 | tf_op jit(solution)/shard_map/rhgd,thd->rhgt/dot_general | solution.py:42
  94.5 0.2 fusion.20
  94.7 1.2 %fusion.16 = bf16[128,1,8,128]{0,3,2,1:T(8,128)(2,1)S(1)} fusion(f32[128,1,8,256]{0,3,2,1:T(8,128)S(1)} %get-tuple-element.18, f32[128,8]{0,1:T(8,128)S(1)} %fusion.60, pred[128,256]{0,1:T(8,128)(4,1)S(1)} %fusion.42, f32[128,8]{0,1:T(8,128)S(1)} %get-tuple-element.12, f32[128,128]{0,1:T(8,128)S(1)} %copy-done.1, f32[128,8]{0,1:T(8,128)S(1)} %get-tuple-element.11, ...), kind=kOutput, calls=%fused_computation.18 | convolution fusion | flops 68419584 | bytes 1486856 | tf_op jit(solution)/shard_map/rhgt,thd->rhgd/dot_general | solution.py:55
  95.9 0.9 copy.83
  (37 shorter events, 1.2 us)
Async XLA Ops:
  6.5 6.1 %copy-start = (bf16[128,8192]{1,0:T(8,128)(2,1)S(1)}, bf16[128,8192]{1,0:T(8,128)(2,1)}, u32[]{:S(2)}) copy-start(bf16[128,8192]{1,0:T(8,128)(2,1)} %param.9) | copy-start | bytes 6291460
  6.5 19.9 %copy-start.2 = (s32[128,8]{0,1:T(8,128)S(1)}, s32[128,8]{0,1:T(8,128)}, u32[]{:S(2)}) copy-start(s32[128,8]{0,1:T(8,128)} %param.15) | copy-start | bytes 12292
  6.5 86.7 %all-gather.2.cloned.1.call-start = ((), (), s32[]{:S(2)}) async-start(), calls=%async_computation.2 | async-start | bytes 1179648 | tf_op jit(solution)/shard_map/all_gather | solution.py:100
  14.6 18.6 %all-to-all-start = ((bf16[16,16,1024]{2,1,0:T(8,128)(2,1)}), bf16[16,16,1024]{2,1,0:T(8,128)(2,1)S(1)}, u32[]{:S(2)}, u32[]{:S(2)}) async-start(bf16[16,16,1024]{2,1,0:T(8,128)(2,1)} %bitcast.10), calls=%async_computation | async-start | bytes 1048576 | tf_op jit(solution)/shard_map/all_to_all | solution.py:110
  62.0 6.8 %copy-start.3 = (s32[128]{0:T(128)S(1)}, s32[128]{0:T(128)}, u32[]{:S(2)}) copy-start(s32[128]{0:T(128)} %param.16) | copy-start | bytes 1540
  65.0 14.6 %all-to-all-start.1 = ((bf16[16,16,1,1280]{3,1,2,0:T(8,128)(2,1)}), bf16[16,16,1,1280]{3,1,2,0:T(8,128)(2,1)S(1)}, u32[]{:S(2)}, u32[]{:S(2)}) async-start(bf16[16,16,1,1280]{3,1,2,0:T(8,128)(2,1)} %fusion.6), calls=%async_computation.1 | async-start | bytes 1310720 | tf_op jit(solution)/shard_map/all_to_all | solution.py:137
  92.8 1.9 %copy-start.1 = (f32[128,128]{0,1:T(8,128)S(1)}, f32[128,128]{0,1:T(8,128)}, u32[]{:S(2)}) copy-start(f32[128,128]{0,1:T(8,128)} %copy.82) | copy-start | bytes 196612
Sparse Core Ops, SparseCore 0:
  9.1 26.0 all-gather.1
where the time goes:
time: 104 us
  blocking collectives  26.7 us (26%)
  matrix products  17.5 us (17%)
  waiting for transfers between devices  16.9 us (16%)
  between operations  13.7 us (13%)
  starting transfers between devices  10.9 us (10%)
  other arithmetic  10.2 us (10%)
  local copies, waits for them, and re-layouts  7.7 us (7%)
    psum x1, blocking collectives, body(): shrunk = lax.psum(shrunk_part, 'ctx').astype(jnp.bfloat16)  26.7 us
    all_to_all x1, waiting for transfers between devices, body(): lax.all_to_all(adapter_update, 'store', split_axis=0, concat_axis=0, tile...  10.1 us
    dot_general x1, matrix products, body(): jnp.dot(tokens, joined_weight.reshape(d_model, head_slice * column_list),...  9.86 us
    all_to_all x1, starting transfers between devices, body(): lax.all_to_all(outgoing.reshape(n_store, CAP, width_slice), 'store', spli...  7.12 us
    all_to_all x1, waiting for transfers between devices, body(): lax.all_to_all(outgoing.reshape(n_store, CAP, width_slice), 'store', spli...  6.79 us
    reduce_or x1, other arithmetic, body(): adapter_hot = jnp.any(adapter_hot, axis=1)  4.45 us
    all_to_all x1, starting transfers between devices, body(): lax.all_to_all(adapter_update, 'store', split_axis=0, concat_axis=0, tile...  3.81 us
    dot_general x1, matrix products, body(): jnp.einsum('oxbl,blpj->oxpj', spread_rows, up_weight, preferred_element_t...  2.99 us
  transfers between devices with their start and end apart: 3, of which 2 were waited for; matrix products, arithmetic and copies ran while one was open for 29% of the time, Pallas kernels for 0%

commit v1 on v0

--- a/solution.py
+++ b/solution.py
@@ -127,7 +127,7 @@
         "hbm,gmq->hbgq", received_parts, down_weight, preferred_element_type=jnp.float32
     )
     shrunk_part = jnp.sum(jnp.where(adapter_hot[..., None], value_partial, 0.0), axis=2)
-    shrunk = lax.psum(shrunk_part, "ctx").astype(jnp.bfloat16)
+    shrunk = jnp.sum(lax.all_gather(shrunk_part, "ctx"), axis=0).astype(jnp.bfloat16)
     spread_rows = jnp.where(
         adapter_hot[..., None], shrunk[:, :, None, :], jnp.zeros((), jnp.bfloat16)
     )

time: 104 us -> 95.5 us (0.918)
  blocking collectives: 26.7 us -> 15.2 us
  waiting for transfers between devices: 16.9 us -> 19.7 us
    psum x1 -> x0, blocking collectives: 26.7 us -> none  [body(): shrunk = lax.psum(shrunk_part, 'ctx').astype(jnp.bfloat16)]
    all_gather x0 -> x1, blocking collectives: none -> 15.2 us  [body(): lax.all_gather(shrunk_part, 'ctx')]
    all_to_all x1, waiting for transfers between devices: 10.1 us -> 12.9 us  [body(): lax.all_to_all(adapter_update, 'store', split_axis=0, concat_axis=0, tile...]
  transfers between devices with their start and end apart: 3 -> 3, of which waited for: 2 -> 2; matrix products, arithmetic and copies ran while one was open for 29% -> 32% of each run, Pallas kernels for 0% -> 0%
where the time goes in v1:
time: 95.5 us; the launch traced here: 94.9 us
  waiting for transfers between devices  19.7 us (21%)
  matrix products  17.5 us (18%)
  blocking collectives  15.2 us (16%)
  between operations  13.7 us (14%)
  starting transfers between devices  10.9 us (11%)
  other arithmetic  10.3 us (11%)
  local copies, waits for them, and re-layouts  7.7 us (8%)
    all_gather x1, blocking collectives, body(): lax.all_gather(shrunk_part, 'ctx')  15.2 us
    all_to_all x1, waiting for transfers between devices, body(): lax.all_to_all(adapter_update, 'store', split_axis=0, concat_axis=0, tile...  12.9 us
    dot_general x1, matrix products, body(): jnp.dot(tokens, joined_weight.reshape(d_model, head_slice * column_list),...  9.86 us
    all_to_all x1, starting transfers between devices, body(): lax.all_to_all(outgoing.reshape(n_store, CAP, width_slice), 'store', spli...  7.12 us
    all_to_all x1, waiting for transfers between devices, body(): lax.all_to_all(outgoing.reshape(n_store, CAP, width_slice), 'store', spli...  6.79 us
    reduce_or x1, other arithmetic, body(): adapter_hot = jnp.any(adapter_hot, axis=1)  4.45 us
    all_to_all x1, starting transfers between devices, body(): lax.all_to_all(adapter_update, 'store', split_axis=0, concat_axis=0, tile...  3.77 us
    dot_general x1, matrix products, body(): jnp.einsum('oxbl,blpj->oxpj', spread_rows, up_weight, preferred_element_t...  2.99 us
  transfers between devices with their start and end apart: 3, of which 2 were waited for; matrix products, arithmetic and copies ran while one was open for 32% of the time, Pallas kernels for 0%

profile of v1, /device:TPU:0, one launch (start us, length us, event | category | flops | bytes accessed | tf_op | source)
XLA Modules:
  0.0 94.9 jit_solution(4126861213734665776)
XLA Ops:
  6.5 1.7 %copy.72 = bf16[32,8,256]{2,0,1:T(8,128)(2,1)} copy(bf16[32,8,256]{2,1,0:T(8,128)(2,1)} %param.17) | data formatting | bytes 262144 | tf_op args[8]
  8.3 1.3 %select_reduce_fusion.1 = s32[2048]{0:T(1024)S(1)} fusion(s32[128]{0:T(128)} %param.14, s32[2048]{0:T(1024)} %param.13), kind=kLoop, calls=%fused_computation.25 | loop fusion | flops 784384 | bytes 16896 | tf_op jit(solution)/shard_map/reduce_sum | solution.py:67
  9.8 2.8 %select_reduce_fusion = s32[16,128]{0,1:T(8,128)S(1)} fusion(s32[16,128]{0,1:T(8,128)S(1)} %copy.73), kind=kOutput, calls=%fused_computation.21 | output fusion | flops 4356096 | bytes 16384 | tf_op jit(solution)/shard_map/jit(cumsum)/reduce_window_sum | solution.py:74
  12.7 2.0 %scatter_custom_fusion = bf16[256,1024]{1,0:T(8,128)(2,1)} fusion(s32[128]{0:T(128)S(1)} %fusion.66, bf16[128,8192]{1,0:T(8,128)(2,1)S(1)} %copy-done, s32[]{:T(128)} %constant.35.clone.1, s32[]{:T(128)S(6)} %select_n.75, bf16[]{:T(256)} %constant.73.clone.1), kind=kCustom, calls=%fused_computation.46 | custom fusion | bytes 786442 | tf_op jit(solution)/shard_map/scatter | solution.py:109
  14.6 7.1 %all-to-all-start = ((bf16[16,16,1024]{2,1,0:T(8,128)(2,1)}), bf16[16,16,1024]{2,1,0:T(8,128)(2,1)S(1)}, u32[]{:S(2)}, u32[]{:S(2)}) async-start(bf16[16,16,1024]{2,1,0:T(8,128)(2,1)} %bitcast.10), calls=%async_computation | async-start | bytes 1048576 | tf_op jit(solution)/shard_map/all_to_all | solution.py:110
  21.9 4.4 %and_reduce_fusion = pred[16,16,8]{2,1,0:T(8,128)(4,1)S(1)} fusion(pred[16,128,8]{1,2,0:T(8,128)(4,1)S(1)} %iota_compare_fusion.4, pred[16,128,16]{1,2,0:T(8,128)(4,1)S(1)} %fusion.41), kind=kLoop, calls=%fused_computation.27 | loop fusion | flops 522240 | bytes 51200 | tf_op jit(solution)/shard_map/reduce_or | solution.py:125
  26.5 6.8 %all-to-all-done = bf16[16,16,1024]{2,1,0:T(8,128)(2,1)S(1)} async-done(((bf16[16,16,1024]{2,1,0:T(8,128)(2,1)}), bf16[16,16,1024]{2,1,0:T(8,128)(2,1)S(1)}, u32[]{:S(2)}, u32[]{:S(2)}) %all-to-all-start) | async-done | bytes 524320 | tf_op jit(solution)/shard_map/all_to_all | solution.py:110
  33.3 2.0 %fusion.12 = f32[16,16,64]{2,1,0:T(8,128)S(1)} fusion(bf16[8,1024,64]{1,2,0:T(8,128)(2,1)} %param.11, bf16[16,16,1024]{2,1,0:T(8,128)(2,1)S(1)} %all-to-all-done, pred[16,16,8]{1,2,0:T(8,128)(4,1)S(1)} %copy.75), kind=kOutput, calls=%fused_computation.13 | convolution fusion | flops 268681216 | bytes 1640448 | tf_op jit(solution)/shard_map/hbm,gmq->hbgq/dot_general | solution.py:126
  35.3 15.2 %all-gather = f32[128,16,64]{2,1,0:T(8,128)S(1)} all-gather(f32[16,16,64]{2,1,0:T(8,128)S(1)} %fusion.12), channel_id=2, replica_groups=mesh['store'=16,'ctx'=8] {'ctx'}, dimensions={0}, use_global_device_ids=true | all-gather | bytes 589824 | tf_op jit(solution)/shard_map/all_gather | solution.py:130
  50.5 3.0 %fusion.6 = bf16[16,16,1,1280]{3,1,2,0:T(8,128)(2,1)} fusion(bf16[8,64,1,1280]{3,1,2,0:T(8,128)(2,1)} %param.12, pred[16,16,8]{1,2,0:T(8,128)(4,1)S(1)} %copy.75, bf16[16,16,64]{2,1,0:T(8,128)(2,1)S(1)} %reduce_sum.58), kind=kOutput, calls=%fused_computation.7 | convolution fusion | flops 336003072 | bytes 2000896 | tf_op jit(solution)/shard_map/oxbl,blpj->oxpj/dot_general | solution.py:134
  53.5 3.8 %all-to-all-start.1 = ((bf16[16,16,1,1280]{3,1,2,0:T(8,128)(2,1)}), bf16[16,16,1,1280]{3,1,2,0:T(8,128)(2,1)S(1)}, u32[]{:S(2)}, u32[]{:S(2)}) async-start(bf16[16,16,1,1280]{3,1,2,0:T(8,128)(2,1)} %fusion.6), calls=%async_computation.1 | async-start | bytes 1310720 | tf_op jit(solution)/shard_map/all_to_all | solution.py:137
  57.7 0.3 multiply_cosine_fusion.1
  58.0 12.9 %all-to-all-done.1 = bf16[16,16,1,1280]{3,1,2,0:T(8,128)(2,1)S(1)} async-done(((bf16[16,16,1,1280]{3,1,2,0:T(8,128)(2,1)}), bf16[16,16,1,1280]{3,1,2,0:T(8,128)(2,1)S(1)}, u32[]{:S(2)}, u32[]{:S(2)}) %all-to-all-start.1) | async-done | bytes 655392 | tf_op jit(solution)/shard_map/all_to_all | solution.py:137
  70.9 1.6 %gather_fusion = bf16[128,1280]{1,0:T(8,128)(2,1)} fusion(bf16[256,1280]{1,0:T(8,128)(2,1)S(1)} %bitcast.145, s32[1024]{0:T(1024)S(1)} %pad_clamp_fusion), kind=kCustom, calls=%fused_computation | custom fusion | bytes 655872 | tf_op jit(solution)/shard_map/gather | solution.py:138
  72.5 9.9 %fusion.7 = f32[128,1,1280]{2,0,1:T(8,128)S(1)} fusion(bf16[128,8192]{1,0:T(8,128)(2,1)S(1)} %copy-done, bf16[8192,1,1280]{2,0,1:T(8,128)(2,1)} %param.10, bf16[128,1280]{1,0:T(8,128)(2,1)} %gather_fusion), kind=kOutput, calls=%fused_computation.8 | convolution fusion | flops 2684846080 | bytes 24051712 | tf_op jit(solution)/shard_map/dot_general | solution.py:139
  82.6 0.7 copy.82
  83.3 0.3 fusion.56
  83.7 0.2 fusion.69
  83.9 0.2 fusion.31
  84.3 0.3 fusion.38
  84.6 1.2 %fusion.70 = (f32[128,8]{0,1:T(8,128)S(1)}, f32[128,1,8,256]{0,3,2,1:T(8,128)S(1)}) fusion(bf16[128,8,128]{2,0,1:T(8,128)(2,1)S(1)} %pad_maximum_fusion, bf16[256,8,256]{2,0,1:T(8,128)(2,1)} %all-gather.3.cloned.1.call-done, s32[]{:T(128)S(6)} %select_n.68, pred[128,256]{0,1:T(8,128)(4,1)S(1)} %fusion.42), kind=kOutput, calls=%fused_computation.112 | convolution fusion | flops 67894272 | bytes 1413124 | tf_op jit(solution)/shard_map/rhgd,thd->rhgt/dot_general | solution.py:42
  85.8 0.2 fusion.20
  86.1 1.2 %fusion.16 = bf16[128,1,8,128]{0,3,2,1:T(8,128)(2,1)S(1)} fusion(f32[128,1,8,256]{0,3,2,1:T(8,128)S(1)} %get-tuple-element.18, f32[128,8]{0,1:T(8,128)S(1)} %fusion.60, pred[128,256]{0,1:T(8,128)(4,1)S(1)} %fusion.42, f32[128,8]{0,1:T(8,128)S(1)} %get-tuple-element.12, f32[128,128]{0,1:T(8,128)S(1)} %copy-done.1, f32[128,8]{0,1:T(8,128)S(1)} %get-tuple-element.11, ...), kind=kOutput, calls=%fused_computation.18 | convolution fusion | flops 68419584 | bytes 1486856 | tf_op jit(solution)/shard_map/rhgt,thd->rhgd/dot_general | solution.py:55
  87.2 0.9 copy.83
  (38 shorter events, 1.3 us)
Async XLA Ops:
  6.5 6.1 %copy-start = (bf16[128,8192]{1,0:T(8,128)(2,1)S(1)}, bf16[128,8192]{1,0:T(8,128)(2,1)}, u32[]{:S(2)}) copy-start(bf16[128,8192]{1,0:T(8,128)(2,1)} %param.9) | copy-start | bytes 6291460
  6.5 19.9 %copy-start.2 = (s32[128,8]{0,1:T(8,128)S(1)}, s32[128,8]{0,1:T(8,128)}, u32[]{:S(2)}) copy-start(s32[128,8]{0,1:T(8,128)} %param.15) | copy-start | bytes 12292
  6.5 78.1 %all-gather.3.cloned.1.call-start = ((), (), s32[]{:S(2)}) async-start(), calls=%async_computation.2 | async-start | bytes 1179648 | tf_op jit(solution)/shard_map/all_gather | solution.py:100
  14.6 18.6 %all-to-all-start = ((bf16[16,16,1024]{2,1,0:T(8,128)(2,1)}), bf16[16,16,1024]{2,1,0:T(8,128)(2,1)S(1)}, u32[]{:S(2)}, u32[]{:S(2)}) async-start(bf16[16,16,1024]{2,1,0:T(8,128)(2,1)} %bitcast.10), calls=%async_computation | async-start | bytes 1048576 | tf_op jit(solution)/shard_map/all_to_all | solution.py:110
  50.5 6.8 %copy-start.3 = (s32[128]{0:T(128)S(1)}, s32[128]{0:T(128)}, u32[]{:S(2)}) copy-start(s32[128]{0:T(128)} %param.16) | copy-start | bytes 1540
  53.5 17.4 %all-to-all-start.1 = ((bf16[16,16,1,1280]{3,1,2,0:T(8,128)(2,1)}), bf16[16,16,1,1280]{3,1,2,0:T(8,128)(2,1)S(1)}, u32[]{:S(2)}, u32[]{:S(2)}) async-start(bf16[16,16,1,1280]{3,1,2,0:T(8,128)(2,1)} %fusion.6), calls=%async_computation.1 | async-start | bytes 1310720 | tf_op jit(solution)/shard_map/all_to_all | solution.py:137
  84.1 1.9 %copy-start.1 = (f32[128,128]{0,1:T(8,128)S(1)}, f32[128,128]{0,1:T(8,128)}, u32[]{:S(2)}) copy-start(f32[128,128]{0,1:T(8,128)} %copy.82) | copy-start | bytes 196612
Sparse Core Ops, SparseCore 0:
  9.1 26.0 all-gather.2
